TPU v7x, 512 devices: a whole 4x4x16 slice. The times are simulated.
512 devices in a mesh: src: 32 (over x, y, z_hi), rcv: 16 (over z_lo, core).
Axes of the slice: x: 4, y: 4, z: 16 (z_hi: 2, z_lo: 8; z = z_hi * 8 + z_lo), core: 2. Of those that a mesh axis runs over, the one named last changes fastest.
Arguments:
- observed: bfloat16 [32, 1280, 128, 128], P('src', 'rcv'), may hold values from -6 to 6
- block_row: int32 [32, 1280], P('src', 'rcv'), may hold values from 0 to 31, as said below
- block_col: int32 [32, 1280], P('src', 'rcv'), may hold values from 0 to 15
- live: int32 [32, 16], P('src', 'rcv'), may hold values from 20 to 80, as said below
- row_factor: bfloat16 [131072, 64], P('src'), may hold values from -5 to 5
- col_factor: bfloat16 [32768, 64], P('rcv'), may hold values from -5 to 5
Outputs:
- new_rows: bfloat16 [131072, 64], P('src')
- new_cols: bfloat16 [32768, 64], P('rcv')
Inputs may be any that keep to these rules, and one draw needn't show every extreme that they name: `block_row`: within one device the 80 slots name distinct blocks of its tile. `live`: some device has all 80 slots in use.
All inputs are finite; a program needn't handle non-finite values.
Results may differ from a plain program's by a relative error of at most 0.007.
Values may be sent and summed in bfloat16 or wider, within the bound.
A program may use at most 64 MiB of HBM per device.

v0:
```python
import math

import jax
import jax.numpy as jnp
from jax import lax
from jax.sharding import PartitionSpec as P


def local(observed, block_row, block_col, live, row_factor, col_factor):
    slot_data = observed[0]
    slot_total = slot_data.shape[0]
    block_size = slot_data.shape[1]
    rank_width = row_factor.shape[1]
    row_block_total = row_factor.shape[0] // block_size
    col_block_total = col_factor.shape[0] // block_size
    row_table = row_factor.reshape(row_block_total, block_size, rank_width)
    col_table = col_factor.reshape(col_block_total, block_size, rank_width)
    row_pick = block_row[0][:, None] == jnp.arange(row_block_total, dtype=jnp.int32)[None, :]
    col_pick = block_col[0][:, None] == jnp.arange(col_block_total, dtype=jnp.int32)[None, :]
    row_blocks = jnp.einsum(
        "ks,sar->kar", row_pick.astype(jnp.bfloat16), row_table, preferred_element_type=jnp.float32
    ).astype(jnp.bfloat16)
    col_blocks = jnp.einsum(
        "kc,cbr->kbr", col_pick.astype(jnp.bfloat16), col_table, preferred_element_type=jnp.float32
    ).astype(jnp.bfloat16)
    predicted = jnp.einsum(
        "kar,kbr->kab", row_blocks, col_blocks, preferred_element_type=jnp.float32
    )
    slot_live = jnp.arange(slot_total, dtype=jnp.int32) < live[0, 0]
    residual = jnp.where(
        slot_live[:, None, None], predicted - slot_data.astype(jnp.float32), 0.0
    ).astype(jnp.bfloat16)
    row_terms = jnp.einsum("kab,kbr->kar", residual, col_blocks, preferred_element_type=jnp.float32)
    row_grad = jnp.einsum("ks,kar->sar", row_pick.astype(jnp.float32), row_terms).reshape(
        row_block_total * block_size, rank_width
    )
    row_step = 0.5 / math.sqrt(slot_total * block_size * lax.axis_size("rcv") // row_block_total)
    row_sums = lax.psum(row_grad, "rcv")
    new_rows = (0.9 * row_factor.astype(jnp.float32) - row_step * row_sums).astype(jnp.bfloat16)
    col_terms = jnp.einsum("kab,kar->kbr", residual, row_blocks, preferred_element_type=jnp.float32)
    col_grad = jnp.einsum("kc,kbr->cbr", col_pick.astype(jnp.float32), col_terms).reshape(
        col_block_total * block_size, rank_width
    )
    col_step = 0.5 / math.sqrt(slot_total * block_size * lax.axis_size("src") // col_block_total)
    col_sums = lax.psum(col_grad, "src")
    new_cols = (0.9 * col_factor.astype(jnp.float32) - col_step * col_sums).astype(jnp.bfloat16)
    return (new_rows, new_cols)


def solution(mesh):
    return jax.shard_map(
        local,
        mesh=mesh,
        in_specs=(
            P("src", "rcv", None, None),
            P("src", "rcv"),
            P("src", "rcv"),
            P("src", "rcv"),
            P("src", None),
            P("rcv", None),
        ),
        out_specs=(P("src", None), P("rcv", None)),
        check_vma=False,
    )
```

profile of v0, /device:TPU:1, one launch (start us, length us, event | category | flops | bytes accessed | tf_op | source)
XLA Modules:
  0.0 812.5 jit_solution(6672184415892702241)
XLA Ops:
  7.2 0.0 all-reduce.5.cloned.1.call-start
  7.9 1.0 copy.13
  8.9 0.0 copy-start.3
  8.9 1.1 copy.12
  10.0 0.0 copy-start.5
  10.1 0.5 convolution_convert_fusion.1
  10.6 0.5 convolution_convert_fusion
  11.2 0.6 copy-done.5
  11.8 1.6 fusion.1
  13.4 0.0 copy-done
  13.4 0.8 fusion.9
  14.2 0.8 fusion.2
  15.1 1.0 copy.31
  16.0 0.0 all-reduce.5.cloned.1.call-update
  16.0 0.0 all-reduce.3.cloned.1.call-start
  16.1 3.2 fusion.6
  19.3 0.9 fusion.4
  20.2 0.0 copy-start.2
  20.2 1.6 copy.30
  21.9 0.0 all-reduce.3.cloned.1.call-update
  21.9 558.6 %all-reduce.5.cloned.1.call-done = f32[2048,64]{0,1:T(8,128)} async-done(((f32[2048,64]{0,1:T(8,128)}), f32[2048,64]{0,1:T(8,128)}) %all-reduce.5.cloned.1.call-update) | async-done | bytes 524304 | tf_op jit(solution)/shard_map/psum | solution.py:45
  580.5 1.8 subtract_convert_fusion.1
  582.3 221.1 %all-reduce.3.cloned.1.call-done = f32[4096,64]{0,1:T(8,128)} async-done(((f32[4096,64]{0,1:T(8,128)}), f32[4096,64]{0,1:T(8,128)}) %all-reduce.3.cloned.1.call-update) | async-done | bytes 1048592 | tf_op jit(solution)/shard_map/psum | solution.py:38
  803.5 2.2 subtract_convert_fusion
  (8 shorter events, 0.0 us)
Async XLA Ops:
  7.2 2.9 copy-start.4
  7.2 573.3 %all-reduce.5.cloned.1.call-start = ((), (), s32[]{:S(2)}) async-start(), calls=%async_computation.1 | async-start | bytes 1048576 | tf_op jit(solution)/shard_map/psum | solution.py:45
  8.9 1.7 copy-start.3
  10.0 1.7 copy-start.5
  11.8 1.6 copy-start
  16.0 787.5 %all-reduce.3.cloned.1.call-start = ((), (), s32[]{:S(2)}) async-start(), calls=%async_computation | async-start | bytes 2097152 | tf_op jit(solution)/shard_map/psum | solution.py:38
  20.2 560.3 %copy-start.2 = (bf16[2048,64]{0,1:T(8,128)(2,1)S(1)}, bf16[2048,64]{0,1:T(8,128)(2,1)}, u32[]{:S(2)}) copy-start(bf16[2048,64]{0,1:T(8,128)(2,1)} %param.11) | copy-start | bytes 786436
  21.9 781.6 %copy-start.1 = (bf16[4096,64]{0,1:T(8,128)(2,1)S(1)}, bf16[4096,64]{0,1:T(8,128)(2,1)}, u32[]{:S(2)}) copy-start(bf16[4096,64]{0,1:T(8,128)(2,1)} %param.10) | copy-start | bytes 1572868
Sparse Core Ops, SparseCore 0:
  16.2 564.3 all-reduce.4
  583.4 220.0 all-reduce.2
where the time goes:
time: 813 us
  waiting for transfers between devices  780 us (96%)
  between operations  14.8 us (2%)
  matrix products  8.45 us (1%)
    psum x1, waiting for transfers between devices, local(): col_sums = lax.psum(col_grad, 'src')  559 us
    psum x1, waiting for transfers between devices, local(): row_sums = lax.psum(row_grad, 'rcv')  221 us
  transfers between devices with their start and end apart: 2, of which 2 were waited for; matrix products, arithmetic and copies ran while one was open for 1% of the time, Pallas kernels for 0%

commit v1 on v0

v1 whole, which is shorter than its diff:
```python
import functools
import math

import jax
import jax.numpy as jnp
from jax import lax
from jax.experimental import pallas as pl
from jax.experimental.pallas import tpu as pltpu
from jax.sharding import PartitionSpec as P

MESH = pl.DeviceIdType.MESH
F32 = jnp.float32
BF16 = jnp.bfloat16

BLK = 128
GROUP = 8
XN, YN, ZH = 4, 4, 2
QUAD = 4


def dot(a, b, dims):
    return lax.dot_general(a, b, (dims, ((), ())), preferred_element_type=F32)


def terms_kernel(
    brow, bcol, live, obs_hbm, row_t, col_t, row_out, col_out, row_own, col_own,
    obs, row_tab, row_acc, col_acc, sems,
):
    slots = obs.shape[0]
    n_row, n_col = row_acc.shape[0], col_acc.shape[0]

    def fetch(g):
        part = pl.ds(g * GROUP, GROUP)
        return pltpu.make_async_copy(obs_hbm.at[part], obs.at[part], sems.at[g])

    for g in range(slots // GROUP):
        fetch(g).start()
    row_acc[...] = jnp.zeros_like(row_acc)
    col_acc[...] = jnp.zeros_like(col_acc)
    for i in range(n_row):
        row_tab[i] = row_t[:, i * BLK : (i + 1) * BLK].T
    count = live[0, 0]

    def group(g, carry):
        fetch(g).wait()

        @pl.when(g * GROUP < count)
        def _():
            terms = []
            for u in range(GROUP):
                k = g * GROUP + u
                i, j = brow[0, k], bcol[0, k]
                ct = col_t[:, pl.ds(pl.multiple_of(j * BLK, BLK), BLK)]
                rt = row_t[:, pl.ds(pl.multiple_of(i * BLK, BLK), BLK)]
                pred = dot(row_tab[i], ct, ((1,), (0,)))
                res = pred - obs[k].astype(F32)
                res = jnp.where(k < count, res, 0.0).astype(BF16)
                terms.append((i, j, dot(ct, res, ((1,), (1,))), dot(rt, res, ((1,), (0,)))))
            for i, j, row_term, col_term in terms:
                row_acc[i] += row_term
                col_acc[j] += col_term

        return carry

    lax.fori_loop(0, slots // GROUP, group, 0)
    row_out[...] = row_acc[...].astype(BF16)
    col_out[...] = col_acc[...].astype(BF16)

    src, rcv = lax.axis_index("src"), lax.axis_index("rcv")
    mine = rcv % 2 * (n_row // 2) + rcv // 2 * 2
    for u in range(2):
        part = pl.ds(pl.multiple_of((mine + u) * BLK, BLK), BLK)
        row_own[u] = 0.9 * row_t[:, part].astype(F32)
    part = pl.ds(pl.multiple_of(src // ZH * BLK, BLK), BLK)
    col_own[0] = 0.9 * col_t[:, part].astype(F32)


def sum_kernel(
    row_step, col_step, row_in, col_in, row_own, col_own, row_out, col_out,
    core_buf, far_sum, near_sum, far_buf, near_buf, far_send, far_recv, col_buf, col_send, col_recv,
    send_sems, recv_sems,
):
    src, rcv = lax.axis_index("src"), lax.axis_index("rcv")
    x, y, zh = src // (YN * ZH), src // ZH % YN, src % ZH
    z, c = rcv // 2, rcv % 2
    q, p = z // QUAD, z % QUAD
    b = src // ZH
    half = row_in.shape[0] // 2
    qb = half // 2

    def at(zz, cc):
        return (src, zz * 2 + cc)

    core = at(z, 1 - c)
    far_z = (1 - q) * QUAD + p
    far = at(far_z, c)
    up = [q * QUAD + (p + d) % QUAD for d in range(1, QUAD)]
    down = [(p + QUAD - d) % QUAD for d in range(1, QUAD)]
    mates = [at(m, c) for m in up]
    steps = [(dx, dy) for dx in range(XN) for dy in range(YN) if dx or dy]
    steps.sort(key=lambda s: -(min(s[0], XN - s[0]) + min(s[1], YN - s[1])))
    places = [(x + dx) % XN * YN + (y + dy) % YN for dx, dy in steps]
    peers = [(place * ZH + zh, rcv) for place in places]
    twin = (b * ZH + 1 - zh, rcv)

    barrier = pltpu.get_barrier_semaphore()
    everyone = [core, far, twin] + mates + peers
    for device in everyone:
        pl.semaphore_signal(barrier, inc=1, device_id=device, device_id_type=MESH)
    pl.semaphore_wait(barrier, len(everyone))

    sent = []

    def copy(source, target, number, device):
        return pltpu.make_async_remote_copy(
            src_ref=source, dst_ref=target, send_sem=send_sems.at[number], recv_sem=recv_sems.at[number],
            device_id=device, device_id_type=MESH,
        )

    def send(source, target, number, device):
        one = copy(source, target, number, device)
        one.start()
        sent.append(one)

    def arrive(target, number):
        copy(target, target, number, core).wait_recv()

    CORE, FAR_IN, NEAR_IN, FAR, COL_IN, TWIN, NEAR_OUT, FAR_OUT, RELAY, CORE_OUT, COL_OUT = (
        0, 2, 5, 8, 9, 24, 25, 28, 29, 32, 40,
    )

    for k, quad in enumerate((1 - q, q)):
        send(row_in.at[pl.ds((1 - c) * half + quad * qb, qb)], core_buf.at[k], CORE + k, core)
    for k, (place, peer) in enumerate(zip(places, peers)):
        send(col_in.at[place], col_buf.at[k], COL_IN + k, peer)

    for k, (quad, total, buf, number) in enumerate(
        ((1 - q, far_sum, far_buf, FAR_IN), (q, near_sum, near_buf, NEAR_IN))
    ):
        arrive(core_buf.at[k], CORE + k)
        own = row_in[pl.ds(c * half + quad * qb, qb)].astype(F32)
        total[...] = (own + core_buf[k].astype(F32)).astype(BF16)
        for d in range(QUAD - 1):
            send(total.at[pl.ds((p + d + 1) % QUAD * 2, 2)], buf.at[d], number + d, mates[d])

    acc = far_sum[pl.ds(p * 2, 2)].astype(F32)
    for d in range(QUAD - 1):
        arrive(far_buf.at[d], FAR_IN + d)
        acc += far_buf[d].astype(F32)
    far_send[...] = acc.astype(BF16)
    send(far_send, far_recv, FAR, far)

    acc = col_in[b].astype(F32)
    for k in range(len(peers)):
        arrive(col_buf.at[k], COL_IN + k)
        acc += col_buf[k].astype(F32)
    col_send[...] = acc.astype(BF16)
    send(col_send, col_recv, TWIN, twin)

    acc = near_sum[pl.ds(p * 2, 2)].astype(F32)
    for d in range(QUAD - 1):
        arrive(near_buf.at[d], NEAR_IN + d)
        acc += near_buf[d].astype(F32)
    arrive(far_recv, FAR)
    acc += far_recv[...].astype(F32)

    def blocks(zz, cc):
        return row_out.at[pl.ds(cc * half + zz * 2, 2)]

    mine = blocks(z, c)
    mine[...] = (row_own[...] - row_step * acc).astype(BF16)
    send(mine, mine, FAR_OUT, far)
    for d in range(QUAD - 1):
        send(mine, mine, NEAR_OUT + d, mates[d])
    send(mine, mine, CORE_OUT, core)

    arrive(col_recv, TWIN)
    acc = col_send[...].astype(F32) + col_recv[...].astype(F32)
    col_out[b] = (col_own[0] - col_step * acc).astype(BF16)
    for k, peer in enumerate(peers):
        send(col_out.at[b], col_out.at[b], COL_OUT + k, peer)

    theirs = blocks(far_z, c)
    arrive(theirs, FAR_OUT)
    for d in range(QUAD - 1):
        send(theirs, theirs, RELAY + d, mates[d])
    send(theirs, theirs, CORE_OUT + 1, core)
    spots = [z, far_z]
    for quad, number in ((q, NEAR_OUT), (1 - q, RELAY)):
        for d in range(QUAD - 1):
            spot = quad * QUAD + down[d]
            part = blocks(spot, c)
            arrive(part, number + d)
            send(part, part, CORE_OUT + len(spots), core)
            spots.append(spot)
    for k, (dx, dy) in enumerate(steps):
        place = (x + XN - dx) % XN * YN + (y + YN - dy) % YN
        arrive(col_out.at[place], COL_OUT + k)
    for k, spot in enumerate(spots):
        arrive(blocks(spot, 1 - c), CORE_OUT + k)
    for one in sent:
        one.wait_send()


def local(observed, block_row, block_col, live, row_factor, col_factor):
    slot_data = observed[0]
    slots = slot_data.shape[0]
    rank = row_factor.shape[1]
    n_row, n_col = row_factor.shape[0] // BLK, col_factor.shape[0] // BLK
    row_t, col_t = row_factor.T, col_factor.T
    vmem = pl.BlockSpec(memory_space=pltpu.VMEM)
    smem = pl.BlockSpec(memory_space=pltpu.SMEM)

    row_terms, col_terms, row_own, col_own = pl.pallas_call(
        terms_kernel,
        out_shape=(
            jax.ShapeDtypeStruct((n_row, rank, BLK), BF16),
            jax.ShapeDtypeStruct((n_col, rank, BLK), BF16),
            jax.ShapeDtypeStruct((2, rank, BLK), F32),
            jax.ShapeDtypeStruct((1, rank, BLK), F32),
        ),
        in_specs=[smem, smem, smem, pl.BlockSpec(memory_space=pl.ANY), vmem, vmem],
        out_specs=(vmem,) * 4,
        scratch_shapes=[
            pltpu.VMEM((slots, BLK, BLK), BF16),
            pltpu.VMEM((n_row, BLK, rank), BF16),
            pltpu.VMEM((n_row, rank, BLK), F32),
            pltpu.VMEM((n_col, rank, BLK), F32),
            pltpu.SemaphoreType.DMA((slots // GROUP,)),
        ],
        name="terms",
    )(block_row, block_col, live, slot_data, row_t, col_t)

    row_step = 0.5 / math.sqrt(slots * BLK * lax.axis_size("rcv") // n_row)
    col_step = 0.5 / math.sqrt(slots * BLK * lax.axis_size("src") // n_col)
    copies = 55
    new_rows, new_cols = pl.pallas_call(
        functools.partial(sum_kernel, row_step, col_step),
        out_shape=(
            jax.ShapeDtypeStruct((n_row, rank, BLK), BF16),
            jax.ShapeDtypeStruct((n_col, rank, BLK), BF16),
        ),
        in_specs=[vmem] * 4,
        out_specs=(vmem, vmem),
        scratch_shapes=[
            pltpu.VMEM((2, n_row // 4, rank, BLK), BF16),
            pltpu.VMEM((n_row // 4, rank, BLK), BF16),
            pltpu.VMEM((n_row // 4, rank, BLK), BF16),
            pltpu.VMEM((QUAD - 1, 2, rank, BLK), BF16),
            pltpu.VMEM((QUAD - 1, 2, rank, BLK), BF16),
            pltpu.VMEM((2, rank, BLK), BF16),
            pltpu.VMEM((2, rank, BLK), BF16),
            pltpu.VMEM((XN * YN - 1, rank, BLK), BF16),
            pltpu.VMEM((rank, BLK), BF16),
            pltpu.VMEM((rank, BLK), BF16),
            pltpu.SemaphoreType.DMA((copies,)),
            pltpu.SemaphoreType.DMA((copies,)),
        ],
        compiler_params=pltpu.CompilerParams(collective_id=0, has_side_effects=True),
        name="sums",
    )(row_terms, col_terms, row_own, col_own)

    def whole(blocks):
        return blocks.transpose(1, 0, 2).reshape(rank, -1).T

    return whole(new_rows), whole(new_cols)


def solution(mesh):
    return jax.shard_map(
        local,
        mesh=mesh,
        in_specs=(
            P("src", "rcv", None, None),
            P("src", "rcv"),
            P("src", "rcv"),
            P("src", "rcv"),
            P("src", None),
            P("rcv", None),
        ),
        out_specs=(P("src", None), P("rcv", None)),
        check_vma=False,
    )
```

time: 813 us -> 62.8 us (0.08)
  waiting for transfers between devices: 780 us -> 0 us
  Pallas kernels: 0 us -> 57.6 us
  between operations: 14.8 us -> 1.29 us
  matrix products: 8.45 us -> 0 us
    psum x2 -> x0, waiting for transfers between devices: 780 us -> none  [the longest x1 559 us: local(): col_sums = lax.psum(col_grad, 'src')]
    pallas_call x0 -> x2, Pallas kernels: none -> 57.6 us  [the longest x1 48 us: local(): pl.pallas_call(functools.partial(sum_kernel, row_step, col_step), out_sha...]
    dot_general x7 -> x0, matrix products: 8.45 us -> none  [the longest x1 3.21 us: local(): jnp.einsum('kab,kbr->kar', residual, col_blocks, preferred_element_type=j...]
  transfers between devices with their start and end apart: 2 -> 0, of which waited for: 2 -> 0; matrix products, arithmetic and copies ran while one was open for 1% -> 0% of each run, Pallas kernels for 0% -> 0%
where the time goes in v1:
time: 62.8 us; the launch traced here: 62.5 us
  Pallas kernels  57.6 us (92%)
  local copies, waits for them, and re-layouts  3.59 us (6%)
  between operations  1.29 us (2%)
    pallas_call x1, Pallas kernels, local(): pl.pallas_call(functools.partial(sum_kernel, row_step, col_step), out_sha...  48 us
    pallas_call x1, Pallas kernels, local(): pl.pallas_call(terms_kernel, out_shape=(jax.ShapeDtypeStruct((n_row, rank...  9.58 us
    transpose x2, local copies, waits for them, and re-layouts, whole(): return blocks.transpose(1, 0, 2).reshape(rank, -1).T  3.59 us

profile of v1, /device:TPU:1, one launch (start us, length us, event | category | flops | bytes accessed | tf_op | source)
XLA Modules:
  0.0 62.5 jit_solution(5598260498057111582)
XLA Ops:
  1.3 9.6 %terms.1 = (bf16[32,64,128]{2,1,0:T(8,128)(2,1)}, bf16[16,64,128]{2,1,0:T(8,128)(2,1)}, f32[2,64,128]{2,1,0:T(8,128)}, f32[1,64,128]{2,1,0:T(8,128)}) custom-call(s32[1,80]{1,0:T(1,128)} %brow.1, s32[1,80]{1,0:T(1,128)} %bcol.1, s32[1,1]{1,0:T(1,128)S(6)} %copy.14.live, bf16[80,128,128]{2,1,0:T(8,128)(2,1)} %bitcast.19, bf16[64,4096]{1,0:T(8,128)(2,1)} %bitcast.20, ...), custom_call_target="tpu_custom_call" | custom-call | tf_op jit(solution)/shard_map/terms/pallas_call | solution.py:214
  10.9 48.0 %sums.1 = (bf16[32,64,128]{2,1,0:T(8,128)(2,1)}, bf16[16,64,128]{2,1,0:T(8,128)(2,1)}) custom-call(bf16[32,64,128]{2,1,0:T(8,128)(2,1)} %get-tuple-element.8.row_in, bf16[16,64,128]{2,1,0:T(8,128)(2,1)} %get-tuple-element.9.col_in, f32[2,64,128]{2,1,0:T(8,128)} %get-tuple-element.10.row_own, f32[1,64,128]{2,1,0:T(8,128)} %get-tuple-element.11.col_own), custom_call_target="tpu_custom_call" | custom-call | tf_op jit(solution)/shard_map/sums/pallas_call | solution.py:237
  58.9 1.9 %bitcast_bitcast_fusion = bf16[4096,64]{0,1:T(8,128)(2,1)} fusion(bf16[32,64,128]{2,1,0:T(8,128)(2,1)} %get-tuple-element.12), kind=kLoop, calls=%fused_computation | loop fusion | bytes 1048576 | tf_op jit(solution)/shard_map/transpose | solution.py:264
  60.8 1.7 %bitcast_bitcast_fusion.1 = bf16[2048,64]{0,1:T(8,128)(2,1)} fusion(bf16[16,64,128]{2,1,0:T(8,128)(2,1)} %get-tuple-element.13), kind=kLoop, calls=%fused_computation.1 | loop fusion | bytes 524288 | tf_op jit(solution)/shard_map/transpose | solution.py:264

commit v2 on v1

--- a/solution.py
+++ b/solution.py
@@ -13,7 +13,9 @@
 BF16 = jnp.bfloat16
 
 BLK = 128
-GROUP = 8
+TERMS_LIMIT = 55_200_000
+LIMIT = 16 << 20
+GROUP = 16
 XN, YN, ZH = 4, 4, 2
 QUAD = 4
 
@@ -23,38 +25,56 @@
 
 
 def terms_kernel(
-    brow, bcol, live, obs_hbm, row_t, col_t, row_out, col_out, row_own, col_own,
-    obs, row_tab, row_acc, col_acc, sems,
+    brow_hbm, bcol_hbm, live, obs_hbm, row_hbm, col_hbm, row_out, col_out, row_own, col_own,
+    brow, bcol, row_t, col_t, obs, row_tab, row_acc, col_acc, arg_sems, sems,
 ):
     slots = obs.shape[0]
     n_row, n_col = row_acc.shape[0], col_acc.shape[0]
 
+    args = [
+        pltpu.make_async_copy(source, target, arg_sems.at[k])
+        for k, (source, target) in enumerate(
+            ((brow_hbm, brow), (bcol_hbm, bcol), (row_hbm, row_t), (col_hbm, col_t))
+        )
+    ]
+
     def fetch(g):
         part = pl.ds(g * GROUP, GROUP)
         return pltpu.make_async_copy(obs_hbm.at[part], obs.at[part], sems.at[g])
 
+    for arg in args:
+        arg.start()
     for g in range(slots // GROUP):
         fetch(g).start()
     row_acc[...] = jnp.zeros_like(row_acc)
     col_acc[...] = jnp.zeros_like(col_acc)
+    for arg in args:
+        arg.wait()
     for i in range(n_row):
         row_tab[i] = row_t[:, i * BLK : (i + 1) * BLK].T
     count = live[0, 0]
 
+    def pick(k):
+        i, j = brow[0, k], bcol[0, k]
+        rt = row_t[:, pl.ds(pl.multiple_of(i * BLK, BLK), BLK)]
+        ct = col_t[:, pl.ds(pl.multiple_of(j * BLK, BLK), BLK)]
+        return i, j, rt, ct
+
     def group(g, carry):
         fetch(g).wait()
 
         @pl.when(g * GROUP < count)
         def _():
+            for u in range(GROUP):
+                k = g * GROUP + u
+                i, _, _, ct = pick(k)
+                res = dot(row_tab[i], ct, ((1,), (0,))) - obs[k].astype(F32)
+                obs[k] = jnp.where(k < count, res, 0.0).astype(BF16)
             terms = []
             for u in range(GROUP):
                 k = g * GROUP + u
-                i, j = brow[0, k], bcol[0, k]
-                ct = col_t[:, pl.ds(pl.multiple_of(j * BLK, BLK), BLK)]
-                rt = row_t[:, pl.ds(pl.multiple_of(i * BLK, BLK), BLK)]
-                pred = dot(row_tab[i], ct, ((1,), (0,)))
-                res = pred - obs[k].astype(F32)
-                res = jnp.where(k < count, res, 0.0).astype(BF16)
+                i, j, rt, ct = pick(k)
+                res = obs[k]
                 terms.append((i, j, dot(ct, res, ((1,), (1,))), dot(rt, res, ((1,), (0,)))))
             for i, j, row_term, col_term in terms:
                 row_acc[i] += row_term
@@ -78,7 +98,7 @@
 def sum_kernel(
     row_step, col_step, row_in, col_in, row_own, col_own, row_out, col_out,
     core_buf, far_sum, near_sum, far_buf, near_buf, far_send, far_recv, col_buf, col_send, col_recv,
-    send_sems, recv_sems,
+    twin_in, send_sems, recv_sems,
 ):
     src, rcv = lax.axis_index("src"), lax.axis_index("rcv")
     x, y, zh = src // (YN * ZH), src // ZH % YN, src % ZH
@@ -102,12 +122,14 @@
     places = [(x + dx) % XN * YN + (y + dy) % YN for dx, dy in steps]
     peers = [(place * ZH + zh, rcv) for place in places]
     twin = (b * ZH + 1 - zh, rcv)
+    side = (b * ZH + 1 - zh, far_z * 2 + c)
 
     barrier = pltpu.get_barrier_semaphore()
-    everyone = [core, far, twin] + mates + peers
+    everyone = [core, far, side] + mates + peers
     for device in everyone:
         pl.semaphore_signal(barrier, inc=1, device_id=device, device_id_type=MESH)
     pl.semaphore_wait(barrier, len(everyone))
+    pl.semaphore_signal(twin_in, inc=1, device_id=far, device_id_type=MESH)
 
     sent = []
 
@@ -155,6 +177,7 @@
         arrive(col_buf.at[k], COL_IN + k)
         acc += col_buf[k].astype(F32)
     col_send[...] = acc.astype(BF16)
+    pl.semaphore_wait(twin_in, 1)
     send(col_send, col_recv, TWIN, twin)
 
     acc = near_sum[pl.ds(p * 2, 2)].astype(F32)
@@ -209,7 +232,7 @@
     n_row, n_col = row_factor.shape[0] // BLK, col_factor.shape[0] // BLK
     row_t, col_t = row_factor.T, col_factor.T
     vmem = pl.BlockSpec(memory_space=pltpu.VMEM)
-    smem = pl.BlockSpec(memory_space=pltpu.SMEM)
+    hbm = pl.BlockSpec(memory_space=pl.ANY)
 
     row_terms, col_terms, row_own, col_own = pl.pallas_call(
         terms_kernel,
@@ -219,15 +242,21 @@
             jax.ShapeDtypeStruct((2, rank, BLK), F32),
             jax.ShapeDtypeStruct((1, rank, BLK), F32),
         ),
-        in_specs=[smem, smem, smem, pl.BlockSpec(memory_space=pl.ANY), vmem, vmem],
+        in_specs=[hbm, hbm, pl.BlockSpec(memory_space=pltpu.SMEM), hbm, hbm, hbm],
         out_specs=(vmem,) * 4,
         scratch_shapes=[
+            pltpu.SMEM((1, slots), jnp.int32),
+            pltpu.SMEM((1, slots), jnp.int32),
+            pltpu.VMEM((rank, n_row * BLK), BF16),
+            pltpu.VMEM((rank, n_col * BLK), BF16),
             pltpu.VMEM((slots, BLK, BLK), BF16),
             pltpu.VMEM((n_row, BLK, rank), BF16),
             pltpu.VMEM((n_row, rank, BLK), F32),
             pltpu.VMEM((n_col, rank, BLK), F32),
+            pltpu.SemaphoreType.DMA((4,)),
             pltpu.SemaphoreType.DMA((slots // GROUP,)),
         ],
+        compiler_params=pltpu.CompilerParams(vmem_limit_bytes=TERMS_LIMIT),
         name="terms",
     )(block_row, block_col, live, slot_data, row_t, col_t)
 
@@ -253,10 +282,13 @@
             pltpu.VMEM((XN * YN - 1, rank, BLK), BF16),
             pltpu.VMEM((rank, BLK), BF16),
             pltpu.VMEM((rank, BLK), BF16),
+            pltpu.SemaphoreType.REGULAR,
             pltpu.SemaphoreType.DMA((copies,)),
             pltpu.SemaphoreType.DMA((copies,)),
         ],
-        compiler_params=pltpu.CompilerParams(collective_id=0, has_side_effects=True),
+        compiler_params=pltpu.CompilerParams(
+            collective_id=0, has_side_effects=True, vmem_limit_bytes=LIMIT
+        ),
         name="sums",
     )(row_terms, col_terms, row_own, col_own)
 

time: 62.8 us -> 49.1 us (0.78)
  the two profiles are of different devices: /device:TPU:1 before, /device:TPU:19 now
where the time goes in v2:
time: 49.1 us; the launch traced here: 49 us
  Pallas kernels  43.8 us (89%)
  local copies, waits for them, and re-layouts  3.85 us (8%)
  between operations  1.3 us (3%)
    pallas_call x1, Pallas kernels, local(): pl.pallas_call(functools.partial(sum_kernel, row_step, col_step), out_sha...  40.7 us
    pallas_call x1, Pallas kernels, local(): pl.pallas_call(terms_kernel, out_shape=(jax.ShapeDtypeStruct((n_row, rank...  3.06 us
    unnamed x6, local copies, waits for them, and re-layouts  2.25 us
    transpose x2, local copies, waits for them, and re-layouts, whole(): return blocks.transpose(1, 0, 2).reshape(rank, -1).T  1.6 us

profile of v2, /device:TPU:19, one launch (start us, length us, event | category | flops | bytes accessed | tf_op | source)
XLA Modules:
  0.0 49.0 jit_solution(13404233915159919037)
XLA Ops:
  1.3 0.0 copy-start
  1.3 0.9 %copy-done = bf16[2048,64]{0,1:T(8,128)(2,1)S(1)} copy-done((bf16[2048,64]{0,1:T(8,128)(2,1)S(1)}, bf16[2048,64]{0,1:T(8,128)(2,1)}, u32[]{:S(2)}) %copy-start) | copy-done | bytes 262168
  2.2 0.0 copy-start.1
  2.2 0.7 %copy-done.1 = s32[1,80]{1,0:T(1,128)S(1)} copy-done((s32[1,80]{1,0:T(1,128)S(1)}, s32[1,80]{1,0:T(1,128)}, u32[]{:S(2)}) %copy-start.1) | copy-done | bytes 344
  2.9 0.0 copy-start.2
  2.9 0.7 %copy-done.2 = s32[1,80]{1,0:T(1,128)S(1)} copy-done((s32[1,80]{1,0:T(1,128)S(1)}, s32[1,80]{1,0:T(1,128)}, u32[]{:S(2)}) %copy-start.2) | copy-done | bytes 344
  3.5 3.1 %terms.1 = (bf16[32,64,128]{2,1,0:T(8,128)(2,1)S(1)}, bf16[16,64,128]{2,1,0:T(8,128)(2,1)S(1)}, f32[2,64,128]{2,1,0:T(8,128)S(1)}, f32[1,64,128]{2,1,0:T(8,128)S(1)}) custom-call(s32[1,80]{1,0:T(1,128)S(1)} %copy-done.1, s32[1,80]{1,0:T(1,128)S(1)} %copy-done.2, s32[1,1]{1,0:T(1,128)S(6)} %copy.14.live, bf16[80,128,128]{2,1,0:T(8,128)(2,1)} %bitcast.20, ...), custom_call_target="tpu_custom_call" | custom-call | tf_op jit(solution)/shard_map/terms/pallas_call | solution.py:237
  6.6 40.7 %sums.1 = (bf16[32,64,128]{2,1,0:T(8,128)(2,1)S(1)}, bf16[16,64,128]{2,1,0:T(8,128)(2,1)S(1)}) custom-call(bf16[32,64,128]{2,1,0:T(8,128)(2,1)S(1)} %get-tuple-element.8.row_in, bf16[16,64,128]{2,1,0:T(8,128)(2,1)S(1)} %get-tuple-element.9.col_in, f32[2,64,128]{2,1,0:T(8,128)S(1)} %get-tuple-element.10.row_own, f32[1,64,128]{2,1,0:T(8,128)S(1)} %get-tuple-element.11.col_own), custom_call_target="tpu_custom_call" | custom-call | tf_op jit(solution)/shard_map/sums/pallas_call | solution.py:266
  47.4 0.9 %bitcast_bitcast_fusion = bf16[4096,64]{0,1:T(8,128)(2,1)} fusion(bf16[32,64,128]{2,1,0:T(8,128)(2,1)S(1)} %get-tuple-element.12), kind=kLoop, calls=%fused_computation | loop fusion | bytes 1048576 | tf_op jit(solution)/shard_map/transpose | solution.py:296
  48.2 0.7 %bitcast_bitcast_fusion.1 = bf16[2048,64]{0,1:T(8,128)(2,1)} fusion(bf16[16,64,128]{2,1,0:T(8,128)(2,1)S(1)} %get-tuple-element.13), kind=kLoop, calls=%fused_computation.1 | loop fusion | bytes 524288 | tf_op jit(solution)/shard_map/transpose | solution.py:296
Async XLA Ops:
  1.3 1.0 %copy-start = (bf16[2048,64]{0,1:T(8,128)(2,1)S(1)}, bf16[2048,64]{0,1:T(8,128)(2,1)}, u32[]{:S(2)}) copy-start(bf16[2048,64]{0,1:T(8,128)(2,1)} %param.11) | copy-start | bytes 786436
  2.2 0.7 %copy-start.1 = (s32[1,80]{1,0:T(1,128)S(1)}, s32[1,80]{1,0:T(1,128)}, u32[]{:S(2)}) copy-start(s32[1,80]{1,0:T(1,128)} %brow_hbm.1) | copy-start | bytes 964
  2.9 0.7 %copy-start.2 = (s32[1,80]{1,0:T(1,128)S(1)}, s32[1,80]{1,0:T(1,128)}, u32[]{:S(2)}) copy-start(s32[1,80]{1,0:T(1,128)} %bcol_hbm.1) | copy-start | bytes 964

commit v3 on v2

--- a/solution.py
+++ b/solution.py
@@ -13,7 +13,6 @@
 BF16 = jnp.bfloat16
 
 BLK = 128
-TERMS_LIMIT = 55_200_000
 LIMIT = 16 << 20
 GROUP = 16
 XN, YN, ZH = 4, 4, 2
@@ -143,29 +142,43 @@
         one = copy(source, target, number, device)
         one.start()
         sent.append(one)
+        return one
+
+    def leave(ones):
+        for one in ones:
+            one.wait_send()
+        sent[:] = [one for one in sent if not any(one is other for other in ones)]
 
     def arrive(target, number):
         copy(target, target, number, core).wait_recv()
 
-    CORE, FAR_IN, NEAR_IN, FAR, COL_IN, TWIN, NEAR_OUT, FAR_OUT, RELAY, CORE_OUT, COL_OUT = (
-        0, 2, 5, 8, 9, 24, 25, 28, 29, 32, 40,
-    )
-
-    for k, quad in enumerate((1 - q, q)):
-        send(row_in.at[pl.ds((1 - c) * half + quad * qb, qb)], core_buf.at[k], CORE + k, core)
+    CORE_FAR, CORE_NEAR, FAR_IN, NEAR_IN, FAR, COL_IN, TWIN = 0, 4, 5, 8, 11, 12, 27
+    NEAR_OUT, FAR_OUT, RELAY, CORE_OUT, COL_OUT = 28, 31, 32, 35, 43
+
+    for d in range(QUAD):
+        spot = (1 - q) * QUAD + (p + d + 1) % QUAD
+        send(row_in.at[pl.ds((1 - c) * half + spot * 2, 2)], core_buf.at[0, pl.ds(d * 2, 2)], CORE_FAR + d, core)
+    send(row_in.at[pl.ds((1 - c) * half + q * qb, qb)], core_buf.at[1], CORE_NEAR, core)
     for k, (place, peer) in enumerate(zip(places, peers)):
         send(col_in.at[place], col_buf.at[k], COL_IN + k, peer)
 
-    for k, (quad, total, buf, number) in enumerate(
-        ((1 - q, far_sum, far_buf, FAR_IN), (q, near_sum, near_buf, NEAR_IN))
-    ):
-        arrive(core_buf.at[k], CORE + k)
-        own = row_in[pl.ds(c * half + quad * qb, qb)].astype(F32)
-        total[...] = (own + core_buf[k].astype(F32)).astype(BF16)
-        for d in range(QUAD - 1):
-            send(total.at[pl.ds((p + d + 1) % QUAD * 2, 2)], buf.at[d], number + d, mates[d])
-
-    acc = far_sum[pl.ds(p * 2, 2)].astype(F32)
+    first = []
+    for d in range(QUAD):
+        part = pl.ds(d * 2, 2)
+        spot = (1 - q) * QUAD + (p + d + 1) % QUAD
+        arrive(core_buf.at[0, part], CORE_FAR + d)
+        own = row_in[pl.ds(c * half + spot * 2, 2)].astype(F32)
+        far_sum[part] = (own + core_buf[0, part].astype(F32)).astype(BF16)
+        if d < QUAD - 1:
+            first.append(send(far_sum.at[part], far_buf.at[d], FAR_IN + d, mates[d]))
+    arrive(core_buf.at[1], CORE_NEAR)
+    own = row_in[pl.ds(c * half + q * qb, qb)].astype(F32)
+    near_sum[...] = (own + core_buf[1].astype(F32)).astype(BF16)
+    leave(first)
+    for d in range(QUAD - 1):
+        send(near_sum.at[pl.ds((p + d + 1) % QUAD * 2, 2)], near_buf.at[d], NEAR_IN + d, mates[d])
+
+    acc = far_sum[pl.ds(QUAD * 2 - 2, 2)].astype(F32)
     for d in range(QUAD - 1):
         arrive(far_buf.at[d], FAR_IN + d)
         acc += far_buf[d].astype(F32)
@@ -192,7 +205,7 @@
 
     mine = blocks(z, c)
     mine[...] = (row_own[...] - row_step * acc).astype(BF16)
-    send(mine, mine, FAR_OUT, far)
+    leave([send(mine, mine, FAR_OUT, far)])
     for d in range(QUAD - 1):
         send(mine, mine, NEAR_OUT + d, mates[d])
     send(mine, mine, CORE_OUT, core)
@@ -234,6 +247,7 @@
     vmem = pl.BlockSpec(memory_space=pltpu.VMEM)
     hbm = pl.BlockSpec(memory_space=pl.ANY)
 
+    fixed = functools.partial(pltpu.with_memory_space_constraint, memory_space=pltpu.HBM)
     row_terms, col_terms, row_own, col_own = pl.pallas_call(
         terms_kernel,
         out_shape=(
@@ -256,13 +270,13 @@
             pltpu.SemaphoreType.DMA((4,)),
             pltpu.SemaphoreType.DMA((slots // GROUP,)),
         ],
-        compiler_params=pltpu.CompilerParams(vmem_limit_bytes=TERMS_LIMIT),
+        compiler_params=pltpu.CompilerParams(vmem_limit_bytes=LIMIT),
         name="terms",
-    )(block_row, block_col, live, slot_data, row_t, col_t)
+    )(fixed(block_row), fixed(block_col), live, fixed(slot_data), fixed(row_t), fixed(col_t))
 
     row_step = 0.5 / math.sqrt(slots * BLK * lax.axis_size("rcv") // n_row)
     col_step = 0.5 / math.sqrt(slots * BLK * lax.axis_size("src") // n_col)
-    copies = 55
+    copies = 58
     new_rows, new_cols = pl.pallas_call(
         functools.partial(sum_kernel, row_step, col_step),
         out_shape=(

time: 49.1 us -> 46.2 us (0.941)
  the two profiles are of different devices: /device:TPU:19 before, /device:TPU:1 now
where the time goes in v3:
time: 46.2 us; the launch traced here: 45.7 us
  Pallas kernels  42.8 us (93%)
  local copies, waits for them, and re-layouts  1.6 us (3%)
  between operations  1.29 us (3%)
    pallas_call x1, Pallas kernels, local(): pl.pallas_call(functools.partial(sum_kernel, row_step, col_step), out_sha...  37.6 us
    pallas_call x1, Pallas kernels, local(): pl.pallas_call(terms_kernel, out_shape=(jax.ShapeDtypeStruct((n_row, rank...  5.2 us
    transpose x2, local copies, waits for them, and re-layouts, whole(): return blocks.transpose(1, 0, 2).reshape(rank, -1).T  1.6 us

profile of v3, /device:TPU:1, one launch (start us, length us, event | category | flops | bytes accessed | tf_op | source)
XLA Modules:
  0.0 45.7 jit_solution(2702534528970216907)
XLA Ops:
  1.3 5.2 %terms.1 = (bf16[32,64,128]{2,1,0:T(8,128)(2,1)S(1)}, bf16[16,64,128]{2,1,0:T(8,128)(2,1)S(1)}, f32[2,64,128]{2,1,0:T(8,128)S(1)}, f32[1,64,128]{2,1,0:T(8,128)S(1)}) custom-call(s32[1,80]{1,0:T(1,128)} %brow_hbm.1, s32[1,80]{1,0:T(1,128)} %bcol_hbm.1, s32[1,1]{1,0:T(1,128)S(6)} %copy.14.live, bf16[80,128,128]{2,1,0:T(8,128)(2,1)} %bitcast.19, ...), custom_call_target="tpu_custom_call" | custom-call | tf_op jit(solution)/shard_map/terms/pallas_call | solution.py:251
  6.5 37.6 %sums.1 = (bf16[32,64,128]{2,1,0:T(8,128)(2,1)S(1)}, bf16[16,64,128]{2,1,0:T(8,128)(2,1)S(1)}) custom-call(bf16[32,64,128]{2,1,0:T(8,128)(2,1)S(1)} %get-tuple-element.8.row_in, bf16[16,64,128]{2,1,0:T(8,128)(2,1)S(1)} %get-tuple-element.9.col_in, f32[2,64,128]{2,1,0:T(8,128)S(1)} %get-tuple-element.10.row_own, f32[1,64,128]{2,1,0:T(8,128)S(1)} %get-tuple-element.11.col_own), custom_call_target="tpu_custom_call" | custom-call | tf_op jit(solution)/shard_map/sums/pallas_call | solution.py:280
  44.1 0.9 %bitcast_bitcast_fusion = bf16[4096,64]{0,1:T(8,128)(2,1)} fusion(bf16[32,64,128]{2,1,0:T(8,128)(2,1)S(1)} %get-tuple-element.12), kind=kLoop, calls=%fused_computation | loop fusion | bytes 1048576 | tf_op jit(solution)/shard_map/transpose | solution.py:310
  45.0 0.7 %bitcast_bitcast_fusion.1 = bf16[2048,64]{0,1:T(8,128)(2,1)} fusion(bf16[16,64,128]{2,1,0:T(8,128)(2,1)S(1)} %get-tuple-element.13), kind=kLoop, calls=%fused_computation.1 | loop fusion | bytes 524288 | tf_op jit(solution)/shard_map/transpose | solution.py:310

commit v4 on v3

--- a/solution.py
+++ b/solution.py
@@ -152,38 +152,45 @@
     def arrive(target, number):
         copy(target, target, number, core).wait_recv()
 
-    CORE_FAR, CORE_NEAR, FAR_IN, NEAR_IN, FAR, COL_IN, TWIN = 0, 4, 5, 8, 11, 12, 27
-    NEAR_OUT, FAR_OUT, RELAY, CORE_OUT, COL_OUT = 28, 31, 32, 35, 43
-
-    for d in range(QUAD):
-        spot = (1 - q) * QUAD + (p + d + 1) % QUAD
-        send(row_in.at[pl.ds((1 - c) * half + spot * 2, 2)], core_buf.at[0, pl.ds(d * 2, 2)], CORE_FAR + d, core)
+    CORE_FAR, CORE_NEAR, FAR_IN, NEAR_IN, FAR, COL_IN, TWIN = 0, 8, 9, 15, 18, 20, 35
+    NEAR_OUT, FAR_OUT, RELAY, CORE_OUT, COL_OUT = 36, 39, 41, 47, 59
+
+    def far_block(h, d):
+        return ((1 - q) * QUAD + (p + d + 1) % QUAD) * 2 + h
+
+    for h in range(2):
+        for d in range(QUAD):
+            k = h * QUAD + d
+            send(row_in.at[(1 - c) * half + far_block(h, d)], core_buf.at[0, k], CORE_FAR + k, core)
     send(row_in.at[pl.ds((1 - c) * half + q * qb, qb)], core_buf.at[1], CORE_NEAR, core)
     for k, (place, peer) in enumerate(zip(places, peers)):
         send(col_in.at[place], col_buf.at[k], COL_IN + k, peer)
 
     first = []
-    for d in range(QUAD):
-        part = pl.ds(d * 2, 2)
-        spot = (1 - q) * QUAD + (p + d + 1) % QUAD
-        arrive(core_buf.at[0, part], CORE_FAR + d)
-        own = row_in[pl.ds(c * half + spot * 2, 2)].astype(F32)
-        far_sum[part] = (own + core_buf[0, part].astype(F32)).astype(BF16)
-        if d < QUAD - 1:
-            first.append(send(far_sum.at[part], far_buf.at[d], FAR_IN + d, mates[d]))
+    for h in range(2):
+        for d in range(QUAD):
+            k = h * QUAD + d
+            arrive(core_buf.at[0, k], CORE_FAR + k)
+            own = row_in[c * half + far_block(h, d)].astype(F32)
+            far_sum[k] = (own + core_buf[0, k].astype(F32)).astype(BF16)
+            if d < QUAD - 1:
+                first.append(send(far_sum.at[k], far_buf.at[d, h], FAR_IN + d * 2 + h, mates[d]))
     arrive(core_buf.at[1], CORE_NEAR)
     own = row_in[pl.ds(c * half + q * qb, qb)].astype(F32)
     near_sum[...] = (own + core_buf[1].astype(F32)).astype(BF16)
-    leave(first)
-    for d in range(QUAD - 1):
-        send(near_sum.at[pl.ds((p + d + 1) % QUAD * 2, 2)], near_buf.at[d], NEAR_IN + d, mates[d])
-
-    acc = far_sum[pl.ds(QUAD * 2 - 2, 2)].astype(F32)
-    for d in range(QUAD - 1):
-        arrive(far_buf.at[d], FAR_IN + d)
-        acc += far_buf[d].astype(F32)
-    far_send[...] = acc.astype(BF16)
-    send(far_send, far_recv, FAR, far)
+
+    for h in range(2):
+        acc = far_sum[h * QUAD + QUAD - 1].astype(F32)
+        for d in range(QUAD - 1):
+            arrive(far_buf.at[d, h], FAR_IN + d * 2 + h)
+            acc += far_buf[d, h].astype(F32)
+        far_send[h] = acc.astype(BF16)
+        send(far_send.at[h], far_recv.at[h], FAR + h, far)
+        if h == 0:
+            leave(first)
+            for d in range(QUAD - 1):
+                part = pl.ds((p + d + 1) % QUAD * 2, 2)
+                send(near_sum.at[part], near_buf.at[d], NEAR_IN + d, mates[d])
 
     acc = col_in[b].astype(F32)
     for k in range(len(peers)):
@@ -193,19 +200,22 @@
     pl.semaphore_wait(twin_in, 1)
     send(col_send, col_recv, TWIN, twin)
 
-    acc = near_sum[pl.ds(p * 2, 2)].astype(F32)
+    near = near_sum[pl.ds(p * 2, 2)].astype(F32)
     for d in range(QUAD - 1):
         arrive(near_buf.at[d], NEAR_IN + d)
-        acc += near_buf[d].astype(F32)
-    arrive(far_recv, FAR)
-    acc += far_recv[...].astype(F32)
+        near += near_buf[d].astype(F32)
 
     def blocks(zz, cc):
         return row_out.at[pl.ds(cc * half + zz * 2, 2)]
 
     mine = blocks(z, c)
-    mine[...] = (row_own[...] - row_step * acc).astype(BF16)
-    leave([send(mine, mine, FAR_OUT, far)])
+    first = []
+    for h in range(2):
+        arrive(far_recv.at[h], FAR + h)
+        acc = near[h] + far_recv[h].astype(F32)
+        mine[h] = (row_own[h] - row_step * acc).astype(BF16)
+        first.append(send(mine.at[h], mine.at[h], FAR_OUT + h, far))
+    leave(first)
     for d in range(QUAD - 1):
         send(mine, mine, NEAR_OUT + d, mates[d])
     send(mine, mine, CORE_OUT, core)
@@ -216,24 +226,33 @@
     for k, peer in enumerate(peers):
         send(col_out.at[b], col_out.at[b], COL_OUT + k, peer)
 
-    theirs = blocks(far_z, c)
-    arrive(theirs, FAR_OUT)
+    parts = [blocks(z, 1 - c)]
+
+    def share(view):
+        one = view(c)
+        send(one, one, CORE_OUT + len(parts), core)
+        parts.append(view(1 - c))
+
+    for h in range(2):
+        one = blocks(far_z, c).at[h]
+        arrive(one, FAR_OUT + h)
+        for d in range(QUAD - 1):
+            send(one, one, RELAY + h * 3 + d, mates[d])
+        share(lambda cc: blocks(far_z, cc).at[h])
     for d in range(QUAD - 1):
-        send(theirs, theirs, RELAY + d, mates[d])
-    send(theirs, theirs, CORE_OUT + 1, core)
-    spots = [z, far_z]
-    for quad, number in ((q, NEAR_OUT), (1 - q, RELAY)):
+        spot = q * QUAD + down[d]
+        arrive(blocks(spot, c), NEAR_OUT + d)
+        share(lambda cc: blocks(spot, cc))
+    for h in range(2):
         for d in range(QUAD - 1):
-            spot = quad * QUAD + down[d]
-            part = blocks(spot, c)
-            arrive(part, number + d)
-            send(part, part, CORE_OUT + len(spots), core)
-            spots.append(spot)
+            spot = (1 - q) * QUAD + down[d]
+            arrive(blocks(spot, c).at[h], RELAY + h * 3 + d)
+            share(lambda cc: blocks(spot, cc).at[h])
     for k, (dx, dy) in enumerate(steps):
         place = (x + XN - dx) % XN * YN + (y + YN - dy) % YN
         arrive(col_out.at[place], COL_OUT + k)
-    for k, spot in enumerate(spots):
-        arrive(blocks(spot, 1 - c), CORE_OUT + k)
+    for k, part in enumerate(parts):
+        arrive(part, CORE_OUT + k)
     for one in sent:
         one.wait_send()
 
@@ -276,7 +295,7 @@
 
     row_step = 0.5 / math.sqrt(slots * BLK * lax.axis_size("rcv") // n_row)
     col_step = 0.5 / math.sqrt(slots * BLK * lax.axis_size("src") // n_col)
-    copies = 58
+    copies = 74
     new_rows, new_cols = pl.pallas_call(
         functools.partial(sum_kernel, row_step, col_step),
         out_shape=(

time: 46.2 us -> 46.9 us (1.015)
  Pallas kernels: 42.8 us -> 43.9 us
    pallas_call x1, Pallas kernels: 37.6 us -> 38.7 us  [local(): pl.pallas_call(functools.partial(sum_kernel, row_step, col_step), out_sha...]
where the time goes in v4:
time: 46.9 us; the launch traced here: 46.8 us
  Pallas kernels  43.9 us (94%)
  local copies, waits for them, and re-layouts  1.6 us (3%)
  between operations  1.29 us (3%)
    pallas_call x1, Pallas kernels, local(): pl.pallas_call(functools.partial(sum_kernel, row_step, col_step), out_sha...  38.7 us
    pallas_call x1, Pallas kernels, local(): pl.pallas_call(terms_kernel, out_shape=(jax.ShapeDtypeStruct((n_row, rank...  5.19 us
    transpose x2, local copies, waits for them, and re-layouts, whole(): return blocks.transpose(1, 0, 2).reshape(rank, -1).T  1.6 us

profile of v4, /device:TPU:1, one launch (start us, length us, event | category | flops | bytes accessed | tf_op | source)
XLA Modules:
  0.0 46.8 jit_solution(6131663478346044942)
XLA Ops:
  1.3 5.2 %terms.1 = (bf16[32,64,128]{2,1,0:T(8,128)(2,1)S(1)}, bf16[16,64,128]{2,1,0:T(8,128)(2,1)S(1)}, f32[2,64,128]{2,1,0:T(8,128)S(1)}, f32[1,64,128]{2,1,0:T(8,128)S(1)}) custom-call(s32[1,80]{1,0:T(1,128)} %brow_hbm.1, s32[1,80]{1,0:T(1,128)} %bcol_hbm.1, s32[1,1]{1,0:T(1,128)S(6)} %copy.14.live, bf16[80,128,128]{2,1,0:T(8,128)(2,1)} %bitcast.19, ...), custom_call_target="tpu_custom_call" | custom-call | tf_op jit(solution)/shard_map/terms/pallas_call | solution.py:270
  6.5 38.7 %sums.1 = (bf16[32,64,128]{2,1,0:T(8,128)(2,1)S(1)}, bf16[16,64,128]{2,1,0:T(8,128)(2,1)S(1)}) custom-call(bf16[32,64,128]{2,1,0:T(8,128)(2,1)S(1)} %get-tuple-element.8.row_in, bf16[16,64,128]{2,1,0:T(8,128)(2,1)S(1)} %get-tuple-element.9.col_in, f32[2,64,128]{2,1,0:T(8,128)S(1)} %get-tuple-element.10.row_own, f32[1,64,128]{2,1,0:T(8,128)S(1)} %get-tuple-element.11.col_own), custom_call_target="tpu_custom_call" | custom-call | tf_op jit(solution)/shard_map/sums/pallas_call | solution.py:299
  45.2 0.9 %bitcast_bitcast_fusion = bf16[4096,64]{0,1:T(8,128)(2,1)} fusion(bf16[32,64,128]{2,1,0:T(8,128)(2,1)S(1)} %get-tuple-element.12), kind=kLoop, calls=%fused_computation | loop fusion | bytes 1048576 | tf_op jit(solution)/shard_map/transpose | solution.py:329
  46.1 0.7 %bitcast_bitcast_fusion.1 = bf16[2048,64]{0,1:T(8,128)(2,1)} fusion(bf16[16,64,128]{2,1,0:T(8,128)(2,1)S(1)} %get-tuple-element.13), kind=kLoop, calls=%fused_computation.1 | loop fusion | bytes 524288 | tf_op jit(solution)/shard_map/transpose | solution.py:329

commit v5 on v4

--- a/solution.py
+++ b/solution.py
@@ -205,16 +205,23 @@
         arrive(near_buf.at[d], NEAR_IN + d)
         near += near_buf[d].astype(F32)
 
-    def blocks(zz, cc):
-        return row_out.at[pl.ds(cc * half + zz * 2, 2)]
-
-    mine = blocks(z, c)
+    def lanes(out, block, count=1):
+        return out.at[:, pl.ds(pl.multiple_of(block * BLK, BLK), count * BLK)]
+
+    def pair(zz, cc):
+        return lanes(row_out, cc * half + zz * 2, 2)
+
+    def single(zz, cc, h):
+        return lanes(row_out, cc * half + zz * 2 + h)
+
+    mine = pair(z, c)
     first = []
     for h in range(2):
         arrive(far_recv.at[h], FAR + h)
         acc = near[h] + far_recv[h].astype(F32)
-        mine[h] = (row_own[h] - row_step * acc).astype(BF16)
-        first.append(send(mine.at[h], mine.at[h], FAR_OUT + h, far))
+        one = single(z, c, h)
+        one[...] = (row_own[h] - row_step * acc).astype(BF16)
+        first.append(send(one, one, FAR_OUT + h, far))
     leave(first)
     for d in range(QUAD - 1):
         send(mine, mine, NEAR_OUT + d, mates[d])
@@ -222,11 +229,12 @@
 
     arrive(col_recv, TWIN)
     acc = col_send[...].astype(F32) + col_recv[...].astype(F32)
-    col_out[b] = (col_own[0] - col_step * acc).astype(BF16)
+    col_mine = lanes(col_out, b)
+    col_mine[...] = (col_own[0] - col_step * acc).astype(BF16)
     for k, peer in enumerate(peers):
-        send(col_out.at[b], col_out.at[b], COL_OUT + k, peer)
-
-    parts = [blocks(z, 1 - c)]
+        send(col_mine, col_mine, COL_OUT + k, peer)
+
+    parts = [pair(z, 1 - c)]
 
     def share(view):
         one = view(c)
@@ -234,23 +242,23 @@
         parts.append(view(1 - c))
 
     for h in range(2):
-        one = blocks(far_z, c).at[h]
+        one = single(far_z, c, h)
         arrive(one, FAR_OUT + h)
         for d in range(QUAD - 1):
             send(one, one, RELAY + h * 3 + d, mates[d])
-        share(lambda cc: blocks(far_z, cc).at[h])
+        share(lambda cc: single(far_z, cc, h))
     for d in range(QUAD - 1):
         spot = q * QUAD + down[d]
-        arrive(blocks(spot, c), NEAR_OUT + d)
-        share(lambda cc: blocks(spot, cc))
+        arrive(pair(spot, c), NEAR_OUT + d)
+        share(lambda cc: pair(spot, cc))
     for h in range(2):
         for d in range(QUAD - 1):
             spot = (1 - q) * QUAD + down[d]
-            arrive(blocks(spot, c).at[h], RELAY + h * 3 + d)
-            share(lambda cc: blocks(spot, cc).at[h])
+            arrive(single(spot, c, h), RELAY + h * 3 + d)
+            share(lambda cc: single(spot, cc, h))
     for k, (dx, dy) in enumerate(steps):
         place = (x + XN - dx) % XN * YN + (y + YN - dy) % YN
-        arrive(col_out.at[place], COL_OUT + k)
+        arrive(lanes(col_out, place), COL_OUT + k)
     for k, part in enumerate(parts):
         arrive(part, CORE_OUT + k)
     for one in sent:
@@ -299,8 +307,8 @@
     new_rows, new_cols = pl.pallas_call(
         functools.partial(sum_kernel, row_step, col_step),
         out_shape=(
-            jax.ShapeDtypeStruct((n_row, rank, BLK), BF16),
-            jax.ShapeDtypeStruct((n_col, rank, BLK), BF16),
+            jax.ShapeDtypeStruct((rank, n_row * BLK), BF16),
+            jax.ShapeDtypeStruct((rank, n_col * BLK), BF16),
         ),
         in_specs=[vmem] * 4,
         out_specs=(vmem, vmem),
@@ -325,10 +333,7 @@
         name="sums",
     )(row_terms, col_terms, row_own, col_own)
 
-    def whole(blocks):
-        return blocks.transpose(1, 0, 2).reshape(rank, -1).T
-
-    return whole(new_rows), whole(new_cols)
+    return new_rows.T, new_cols.T
 
 
 def solution(mesh):

time: 46.9 us -> 46.5 us (level); the launches traced: 46.8 us -> 45.7 us
  Pallas kernels: 43.9 us -> 42.9 us
    transpose x2 -> x0, local copies, waits for them, and re-layouts: 1.6 us -> none  [whole(): return blocks.transpose(1, 0, 2).reshape(rank, -1).T]
    unnamed x0 -> x2, local copies, waits for them, and re-layouts: none -> 1.5 us
    pallas_call x1, Pallas kernels: 5.19 us -> 4.47 us  [local(): pl.pallas_call(terms_kernel, out_shape=(jax.ShapeDtypeStruct((n_row, rank...]
where the time goes in v5:
time: 46.5 us; the launch traced here: 45.7 us
  Pallas kernels  42.9 us (92%)
  local copies, waits for them, and re-layouts  1.5 us (3%)
  between operations  1.29 us (3%)
    pallas_call x1, Pallas kernels, local(): pl.pallas_call(functools.partial(sum_kernel, row_step, col_step), out_sha...  38.4 us
    pallas_call x1, Pallas kernels, local(): pl.pallas_call(terms_kernel, out_shape=(jax.ShapeDtypeStruct((n_row, rank...  4.47 us
    unnamed x2, local copies, waits for them, and re-layouts  1.5 us

profile of v5, /device:TPU:1, one launch (start us, length us, event | category | flops | bytes accessed | tf_op | source)
XLA Modules:
  0.0 45.7 jit_solution(12467466026814797719)
XLA Ops:
  1.3 4.5 %terms.1 = (bf16[32,64,128]{2,1,0:T(8,128)(2,1)S(1)}, bf16[16,64,128]{2,1,0:T(8,128)(2,1)S(1)}, f32[2,64,128]{2,1,0:T(8,128)S(1)}, f32[1,64,128]{2,1,0:T(8,128)S(1)}) custom-call(s32[1,80]{1,0:T(1,128)} %brow_hbm.1, s32[1,80]{1,0:T(1,128)} %bcol_hbm.1, s32[1,1]{1,0:T(1,128)S(6)} %copy.10.live, bf16[80,128,128]{2,1,0:T(8,128)(2,1)} %bitcast.7, ...), custom_call_target="tpu_custom_call" | custom-call | tf_op jit(solution)/shard_map/terms/pallas_call | solution.py:278
  5.8 38.4 %sums.1 = (bf16[64,4096]{1,0:T(8,128)(2,1)S(1)}, bf16[64,2048]{1,0:T(8,128)(2,1)S(1)}) custom-call(bf16[32,64,128]{2,1,0:T(8,128)(2,1)S(1)} %get-tuple-element.8.row_in, bf16[16,64,128]{2,1,0:T(8,128)(2,1)S(1)} %get-tuple-element.9.col_in, f32[2,64,128]{2,1,0:T(8,128)S(1)} %get-tuple-element.10.row_own, f32[1,64,128]{2,1,0:T(8,128)S(1)} %get-tuple-element.11.col_own), custom_call_target="tpu_custom_call" | custom-call | tf_op jit(solution)/shard_map/sums/pallas_call | solution.py:307
  44.2 0.8 %copy.11 = bf16[4096,64]{0,1:T(8,128)(2,1)} copy(bf16[4096,64]{0,1:T(8,128)(2,1)S(1)} %bitcast.5) | data formatting | bytes 1048576
  45.0 0.7 %copy.12 = bf16[2048,64]{0,1:T(8,128)(2,1)} copy(bf16[2048,64]{0,1:T(8,128)(2,1)S(1)} %bitcast.6) | data formatting | bytes 524288
